TPU v7x, 32 devices: a whole 2x2x4 slice. The times are simulated.
32 devices in a mesh: clip: 8 (over z, core), frame: 4 (over y, x).
Axes of the slice: x: 2, y: 2, z: 4, core: 2. Of those that a mesh axis runs over, the one named last changes fastest.
Arguments:
- block_input: bfloat16 [16, 16, 64, 1152], P('clip', 'frame'), may hold values from -6 to 6
- modulation: bfloat16 [16, 6912], P('clip'), may hold values from -4 to 4
- frame_counts: int32 [16], P('clip'), may hold values from 8 to 16, as said below
- qkv_weight: bfloat16 [1152, 3456], replicated, may hold values from -0.1875 to 0.1875
- qv_bias: bfloat16 [2304], replicated, may hold values from -3 to 3
- out_weight: bfloat16 [1152, 1152], replicated, may hold values from -0.375 to 0.375
- out_bias: bfloat16 [1152], replicated, may hold values from -3 to 3
- fc1_weight: bfloat16 [1152, 4608], replicated, may hold values from -0.1875 to 0.1875
- fc1_bias: bfloat16 [4608], replicated, may hold values from -3 to 3
- fc2_weight: bfloat16 [4608, 1152], replicated, may hold values from -0.09375 to 0.09375
- fc2_bias: bfloat16 [1152], replicated, may hold values from -3 to 3
- out_cotangent: bfloat16 [16, 16, 64, 1152], P('clip', 'frame'), may hold values from -6 to 6
Outputs:
- block_output: bfloat16 [16, 16, 64, 1152], P('clip', 'frame')
- input_grad: bfloat16 [16, 16, 64, 1152], P('clip', 'frame')
- modulation_grad: float32 [16, 6912], P('clip', 'frame')
- qkv_weight_grad: float32 [1152, 3456], P('clip', 'frame')
- qv_bias_grad: float32 [2304], P('frame')
- out_weight_grad: float32 [1152, 1152], P('clip', 'frame')
- out_bias_grad: float32 [1152], P('frame')
- fc1_weight_grad: float32 [1152, 4608], P('clip', 'frame')
- fc1_bias_grad: float32 [4608], P('frame')
- fc2_weight_grad: float32 [4608, 1152], P('clip', 'frame')
- fc2_bias_grad: float32 [1152], P('frame')
Inputs may be any that keep to these rules, and one draw needn't show every extreme that they name: `frame_counts`: each clip holds 8 to 16 frames in its leading slots; some clip holds 16 and some other clip 16 // 2.
All inputs are finite; a program needn't handle non-finite values.
Results may differ from a plain program's by a relative error of at most 0.013.
The roundings to bfloat16 on the way count: a program that leaves them out, or rounds other values in their place, can miss the bound.
Values may be sent and summed in bfloat16 or wider, within the bound.
A program may use at most 256 MiB of HBM per device.

v0:
```python
import jax
import jax.numpy as jnp
from jax import lax
from jax.sharding import PartitionSpec as P

HEADS = 16
EPSILON = 1e-06
NEGATIVE = -1e30


def normalize(values):
    centred = values - jnp.mean(values, axis=-1, keepdims=True)
    variance = jnp.mean(centred * centred, axis=-1, keepdims=True)
    return centred * lax.rsqrt(variance + EPSILON)


def modulate(values, shift_term, scale_term):
    return normalize(values) * (1.0 + scale_term) + shift_term


def gelu_tanh(inputs):
    return jax.nn.gelu(inputs, approximate=True)


def contract_rows(left, right):
    return lax.dot_general(
        left, right, (((0,), (0,)), ((), ())), preferred_element_type=jnp.float32
    )


def contract_cols(left, right):
    return lax.dot_general(
        left, right, (((1,), (1,)), ((), ())), preferred_element_type=jnp.float32
    )


def on_device(
    block_input,
    modulation,
    frame_counts,
    qkv_weight,
    qv_bias,
    out_weight,
    out_bias,
    fc1_weight,
    fc1_bias,
    fc2_weight,
    fc2_bias,
    out_cotangent,
):
    swapped = lax.all_to_all(block_input, "frame", split_axis=2, concat_axis=1, tiled=True)
    clip_count, frames, patches, model_width = swapped.shape
    head_width = model_width // HEADS
    row_count = clip_count * frames * patches
    factor = head_width ** (-0.5)
    frame_valid = (jnp.arange(frames)[None, :] < frame_counts[:, None]).astype(jnp.float32)
    valid_rows = frame_valid[:, :, None, None]
    key_valid = frame_valid[:, None, None, None, :] > 0.5
    modulators = modulation.astype(jnp.float32).reshape(clip_count, 6, model_width)[
        :, :, None, None, :
    ]
    shift_one = modulators[:, 0]
    scale_one = modulators[:, 1]
    gate_one = modulators[:, 2]
    shift_two = modulators[:, 3]
    scale_two = modulators[:, 4]
    gate_two = modulators[:, 5]
    residual = swapped.astype(jnp.float32)
    normed_full, modulate_back_one = jax.vjp(modulate, residual, shift_one, scale_one)
    normed_one = normed_full.astype(jnp.bfloat16).reshape(row_count, model_width)
    bias_full = jnp.concatenate(
        [qv_bias[:model_width], jnp.zeros((model_width,), jnp.bfloat16), qv_bias[model_width:]]
    ).astype(jnp.float32)
    projected = (
        jnp.dot(normed_one, qkv_weight, preferred_element_type=jnp.float32) + bias_full
    ).astype(jnp.bfloat16)
    shaped = projected.reshape(clip_count, frames, patches, 3, HEADS, head_width)
    queries = shaped[:, :, :, 0]
    keys_all = shaped[:, :, :, 1]
    values_all = shaped[:, :, :, 2]
    scores = (
        jnp.einsum("cfphd,cgphd->cphfg", queries, keys_all, preferred_element_type=jnp.float32)
        * factor
    )
    scores = jnp.where(key_valid, scores, NEGATIVE)
    row_peak = jnp.max(scores, axis=-1, keepdims=True)
    exponent = jnp.exp(scores - row_peak)
    attention_weights = exponent / jnp.sum(exponent, axis=-1, keepdims=True)
    weights_low = attention_weights.astype(jnp.bfloat16)
    context = jnp.einsum(
        "cphfg,cgphd->cfphd", weights_low, values_all, preferred_element_type=jnp.float32
    )
    context_low = context.astype(jnp.bfloat16).reshape(row_count, model_width)
    attended = jnp.dot(
        context_low, out_weight, preferred_element_type=jnp.float32
    ) + out_bias.astype(jnp.float32)
    attended = attended.reshape(clip_count, frames, patches, model_width)
    middle = residual + gate_one * attended
    normed_mid, modulate_back_two = jax.vjp(modulate, middle, shift_two, scale_two)
    normed_two = normed_mid.astype(jnp.bfloat16).reshape(row_count, model_width)
    hidden = jnp.dot(normed_two, fc1_weight, preferred_element_type=jnp.float32) + fc1_bias.astype(
        jnp.float32
    )
    activated_full, gelu_back = jax.vjp(gelu_tanh, hidden)
    activated = activated_full.astype(jnp.bfloat16)
    branch_two = jnp.dot(
        activated, fc2_weight, preferred_element_type=jnp.float32
    ) + fc2_bias.astype(jnp.float32)
    branch_two = branch_two.reshape(clip_count, frames, patches, model_width)
    result = valid_rows * (middle + gate_two * branch_two)
    block_output = lax.all_to_all(
        result.astype(jnp.bfloat16), "frame", split_axis=1, concat_axis=2, tiled=True
    )
    cotangent = lax.all_to_all(
        out_cotangent, "frame", split_axis=2, concat_axis=1, tiled=True
    ).astype(jnp.float32)
    d_result = valid_rows * cotangent
    d_gate_two = jnp.sum(d_result * branch_two, axis=(1, 2))
    d_branch = (d_result * gate_two).astype(jnp.bfloat16).reshape(row_count, model_width)
    d_fc2_bias = jnp.sum(d_branch.astype(jnp.float32), axis=0)
    d_fc2_weight = contract_rows(activated, d_branch)
    d_activated = contract_cols(d_branch, fc2_weight)
    d_hidden = gelu_back(d_activated)[0].astype(jnp.bfloat16)
    d_fc1_bias = jnp.sum(d_hidden.astype(jnp.float32), axis=0)
    d_fc1_weight = contract_rows(normed_two, d_hidden)
    d_normed_two = contract_cols(d_hidden, fc1_weight).reshape(
        clip_count, frames, patches, model_width
    )
    d_middle_norm, d_shift_two, d_scale_two = modulate_back_two(d_normed_two)
    d_middle = d_result + d_middle_norm
    d_gate_one = jnp.sum(d_middle * attended, axis=(1, 2))
    d_attended = (d_middle * gate_one).astype(jnp.bfloat16).reshape(row_count, model_width)
    d_out_bias = jnp.sum(d_attended.astype(jnp.float32), axis=0)
    d_out_weight = contract_rows(context_low, d_attended)
    d_context = contract_cols(d_attended, out_weight).astype(jnp.bfloat16)
    d_context = d_context.reshape(clip_count, frames, patches, HEADS, head_width)
    d_weights = jnp.einsum(
        "cfphd,cgphd->cphfg", d_context, values_all, preferred_element_type=jnp.float32
    )
    d_values = jnp.einsum(
        "cphfg,cfphd->cgphd", weights_low, d_context, preferred_element_type=jnp.float32
    )
    d_scores = attention_weights * (
        d_weights - jnp.sum(attention_weights * d_weights, axis=-1, keepdims=True)
    )
    d_scores = d_scores.astype(jnp.bfloat16)
    d_queries = (
        jnp.einsum("cphfg,cgphd->cfphd", d_scores, keys_all, preferred_element_type=jnp.float32)
        * factor
    )
    d_keys = (
        jnp.einsum("cphfg,cfphd->cgphd", d_scores, queries, preferred_element_type=jnp.float32)
        * factor
    )
    d_projected = (
        jnp.stack([d_queries, d_keys, d_values], axis=3)
        .astype(jnp.bfloat16)
        .reshape(row_count, 3 * model_width)
    )
    column_sums = jnp.sum(d_projected.astype(jnp.float32), axis=0)
    d_qv_bias = jnp.concatenate([column_sums[:model_width], column_sums[2 * model_width :]])
    d_qkv_weight = contract_rows(normed_one, d_projected)
    d_normed_one = contract_cols(d_projected, qkv_weight).reshape(
        clip_count, frames, patches, model_width
    )
    d_residual, d_shift_one, d_scale_one = modulate_back_one(d_normed_one)
    d_input = d_middle + d_residual
    input_grad = lax.all_to_all(
        d_input.astype(jnp.bfloat16), "frame", split_axis=1, concat_axis=2, tiled=True
    )
    d_modulation = jnp.stack(
        [
            d_shift_one.reshape(clip_count, model_width),
            d_scale_one.reshape(clip_count, model_width),
            d_gate_one,
            d_shift_two.reshape(clip_count, model_width),
            d_scale_two.reshape(clip_count, model_width),
            d_gate_two,
        ],
        axis=1,
    ).reshape(clip_count, 6 * model_width)
    every_part = (
        lax.psum_scatter(d_qkv_weight, "frame", scatter_dimension=1, tiled=True),
        lax.psum_scatter(d_out_weight, "frame", scatter_dimension=1, tiled=True),
        lax.psum_scatter(d_fc1_weight, "frame", scatter_dimension=1, tiled=True),
        lax.psum_scatter(d_fc2_weight, "frame", scatter_dimension=1, tiled=True),
        lax.psum_scatter(d_modulation, "frame", scatter_dimension=1, tiled=True),
        lax.psum_scatter(d_qv_bias, "frame", scatter_dimension=0, tiled=True),
        lax.psum_scatter(d_out_bias, "frame", scatter_dimension=0, tiled=True),
        lax.psum_scatter(d_fc1_bias, "frame", scatter_dimension=0, tiled=True),
        lax.psum_scatter(d_fc2_bias, "frame", scatter_dimension=0, tiled=True),
    )
    every_mat = (
        lax.psum_scatter(every_part[0], "clip", scatter_dimension=0, tiled=True),
        lax.psum_scatter(every_part[1], "clip", scatter_dimension=0, tiled=True),
        lax.psum_scatter(every_part[2], "clip", scatter_dimension=0, tiled=True),
        lax.psum_scatter(every_part[3], "clip", scatter_dimension=0, tiled=True),
    )
    qkv_grad = every_mat[0]
    out_grad = every_mat[1]
    fc1_grad = every_mat[2]
    fc2_grad = every_mat[3]
    modulation_grad = every_part[4]
    bias_parts = (every_part[5], every_part[6], every_part[7], every_part[8])
    bias_totals = lax.psum((bias_parts[0], bias_parts[1], bias_parts[2], bias_parts[3]), "clip")
    return (
        block_output,
        input_grad,
        modulation_grad,
        qkv_grad,
        bias_totals[0],
        out_grad,
        bias_totals[1],
        fc1_grad,
        bias_totals[2],
        fc2_grad,
        bias_totals[3],
    )


def solution(mesh):
    placed = (
        P("clip", "frame", None, None),
        P("clip", None),
        P("clip"),
        P(),
        P(),
        P(),
        P(),
        P(),
        P(),
        P(),
        P(),
        P("clip", "frame", None, None),
    )
    return jax.shard_map(
        on_device,
        mesh=mesh,
        in_specs=placed,
        out_specs=(
            P("clip", "frame", None, None),
            P("clip", "frame", None, None),
            P("clip", "frame"),
            P("clip", "frame"),
            P("frame"),
            P("clip", "frame"),
            P("frame"),
            P("clip", "frame"),
            P("frame"),
            P("clip", "frame"),
            P("frame"),
        ),
        check_vma=False,
    )
```

profile of v0, /device:TPU:0, one launch (start us, length us, event | category | flops | bytes accessed | tf_op | source)
XLA Modules:
  0.0 1028.3 jit_solution(13910262976260021615)
XLA Ops:
  7.2 3.3 copy.57
  10.6 5.3 all-to-all-start
  16.1 3.2 copy.66
  19.6 12.0 %all-to-all-done = bf16[2,4,64,1152]{3,1,0,2:T(4,128)(2,1)} async-done(((bf16[2,4,64,1152]{3,1,0,2:T(4,128)(2,1)}), bf16[2,4,64,1152]{3,1,0,2:T(4,128)(2,1)}, u32[]{:S(2)}, u32[]{:S(2)}) %all-to-all-start) | async-done | bytes 1179680 | tf_op jit(solution)/shard_map/all_to_all | solution.py:51
  31.6 4.3 all-to-all-start.2
  43.7 10.0 add_convert_fusion
  53.8 13.6 %reshape.417 = bf16[2,16,16,3,16,72]{5,4,3,2,1,0:T(8,128)(2,1)} reshape(bf16[512,3456]{1,0:T(8,128)(2,1)} %add_convert_fusion) | data formatting | bytes 7077888 | tf_op jit(solution)/shard_map/reshape | solution.py:77
  67.4 5.0 fusion.48
  72.4 2.5 fusion.33
  74.9 2.4 fusion.52
  77.3 1.8 convert_bitcast_fusion
  79.2 1.9 copy.63
  81.1 5.1 reshape.418
  86.2 3.3 convolution_add_fusion.1
  89.5 2.2 fusion.47
  91.7 2.0 multiply_reduce_fusion.6
  93.9 1.6 copy.67
  95.9 2.9 fusion.17
  98.9 9.5 fusion.53
  108.7 3.4 copy-done.47
  113.1 10.3 %fusion.42 = f32[4608,1152]{0,1:T(8,128)} fusion(bf16[512,1152]{1,0:T(8,128)(2,1)S(1)} %fusion.19, f32[512,4608]{1,0:T(8,128)S(1)} %fusion.53, f32[4608]{0:T(1024)S(1)} %convert_element_type.207), kind=kOutput, calls=%fused_computation.115 | convolution fusion | flops 5459410944 | bytes 31868928 | tf_op jit(solution)/shard_map/dot_general | solution.py:26
  124.1 15.8 %convert_reduce_fusion.1 = (f32[4608]{0:T(1024)S(1)}, bf16[512,4608]{1,0:T(8,128)(2,1)S(1)}) fusion(f32[512,4608]{1,0:T(8,128)} %copy-done.47, f32[4608]{0:T(1024)S(1)} %convert_element_type.207, bf16[512,1152]{1,0:T(8,128)(2,1)} %copy-done.33, bf16[4608,1152]{1,0:T(8,128)(2,1)} %param.21), kind=kOutput, calls=%fused_computation.12 | convolution fusion | flops 5490077184 | bytes 25989120 | tf_op jit(solution)/shard_map/dot_general | solution.py:32
  139.9 11.1 %fusion.54 = f32[512,1152]{1,0:T(8,128)S(1)} fusion(bf16[512,4608]{1,0:T(8,128)(2,1)S(1)} %get-tuple-element.58, bf16[1152,4608]{1,0:T(8,128)(2,1)} %param.19), kind=kOutput, calls=%fused_computation.126 | convolution fusion | flops 5435817984 | bytes 17694720 | tf_op jit(solution)/shard_map/dot_general | solution.py:32
  153.0 4.3 fusion.46
  158.9 4.1 fusion.56
  163.0 4.2 convolution_convert_fusion
  167.3 5.2 reshape.424
  172.5 7.1 multiply_reduce_fusion
  181.3 1.7 multiply_bitcast_fusion.1
  183.2 1.7 multiply_bitcast_fusion
  184.9 1.6 convolution_bitcast_fusion
  186.5 2.2 convert_reduce_fusion
  188.7 4.2 copy.71
  193.0 11.3 %convert_element_type.223 = bf16[2,16,16,3456]{3,2,1,0:T(8,128)(2,1)} reshape(bf16[2,16,16,3,16,72]{5,4,3,2,1,0:T(8,128)(2,1)} %copy.71) | data formatting | bytes 7077888 | tf_op jit(solution)/shard_map/convert_element_type | solution.py:157
  204.3 11.0 %convert_element_type.227 = bf16[512,3456]{1,0:T(8,128)(2,1)} reshape(bf16[2,16,16,3,16,72]{5,4,3,2,1,0:T(8,128)(2,1)} %copy.71) | data formatting | bytes 7077888 | tf_op jit(solution)/shard_map/convert_element_type | solution.py:157
  215.3 9.8 multiply_reduce_fusion.4
  225.2 2.0 multiply_reduce_fusion.3
  227.2 13.6 %convolution_add_fusion = f32[512,1152]{1,0:T(8,128)S(1)} fusion(bf16[4608,1152]{1,0:T(8,128)(2,1)} %param.21, f32[1152]{0:T(1024)S(1)} %convert_element_type.209, f32[512,4608]{1,0:T(8,128)} %copy-done.47, f32[4608]{0:T(1024)S(1)} %convert_element_type.207), kind=kOutput, calls=%fused_computation.30 | convolution fusion | flops 5460000768 | bytes 22436352 | tf_op jit(solution)/shard_map/dot_general | solution.py:106
  240.9 2.7 multiply_reduce_fusion.2
  243.6 2.1 add_convert_fusion.1
  245.8 8.4 fusion.55
  255.8 12.2 %fusion.57 = f32[1152,4608]{1,0:T(8,128)} fusion(bf16[512,1152]{1,0:T(8,128)(2,1)S(1)} %copy-done.23, bf16[512,4608]{1,0:T(8,128)(2,1)} %copy-done.21), kind=kOutput, calls=%fused_computation.129 | convolution fusion | flops 5435817984 | bytes 27131904 | tf_op jit(solution)/shard_map/dot_general | solution.py:26
  268.3 2.7 copy.88
  271.0 44.4 %reduce-scatter.26.cloned.1.call-done = f32[4608,288]{0,1:T(8,128)} async-done(((f32[4608,1152]{0,1:T(8,128)}), f32[4608,288]{0,1:T(8,128)}) %reduce-scatter.26.cloned.1.call-update) | async-done | bytes 5308432 | tf_op jit(solution)/shard_map/reduce_scatter | solution.py:186
  315.4 6.7 copy.86
  322.2 58.5 %reduce-scatter.20.cloned.1.call-done = f32[1152,288]{0,1:T(8,128)} async-done(((f32[1152,1152]{0,1:T(8,128)}), f32[1152,288]{0,1:T(8,128)}) %reduce-scatter.20.cloned.1.call-update) | async-done | bytes 1327120 | tf_op jit(solution)/shard_map/reduce_scatter | solution.py:184
  380.7 3.1 copy.84
  383.9 147.6 %reduce-scatter.18.cloned.1.call-done = f32[1152,864]{0,1:T(8,128)} async-done(((f32[1152,3456]{0,1:T(8,128)}), f32[1152,864]{0,1:T(8,128)}) %reduce-scatter.18.cloned.1.call-update) | async-done | bytes 3981328 | tf_op jit(solution)/shard_map/reduce_scatter | solution.py:183
  531.5 5.6 copy.82
  537.1 187.3 %reduce-scatter.22.cloned.1.call-done = f32[1152,1152]{1,0:T(8,128)} async-done(((f32[1152,4608]{1,0:T(8,128)}), f32[1152,1152]{1,0:T(8,128)}) %reduce-scatter.22.cloned.1.call-update) | async-done | bytes 5308432 | tf_op jit(solution)/shard_map/reduce_scatter | solution.py:185
  726.8 3.5 all-to-all-start.3
  734.2 21.7 %all-to-all-done.3 = bf16[2,16,16,1152]{3,2,0,1:T(8,128)(2,1)S(1)} async-done(((bf16[2,16,16,1152]{3,2,0,1:T(8,128)(2,1)}), bf16[2,16,16,1152]{3,2,0,1:T(8,128)(2,1)S(1)}, u32[]{:S(2)}, u32[]{:S(2)}) %all-to-all-start.3) | async-done | bytes 1179680 | tf_op jit(solution)/shard_map/all_to_all | solution.py:168
  755.9 4.3 all-to-all-start.1
  760.2 1.6 bitcast_convert_fusion
  762.4 25.4 %all-reduce.5 = (f32[2304]{0:T(1024)S(1)}, f32[1152]{0:T(1024)S(1)}, f32[4608]{0:T(1024)S(1)}, f32[1152]{0:T(1024)S(1)}) all-reduce(f32[2304]{0:T(1024)S(1)} %pad_maximum_fusion, f32[1152]{0:T(1024)S(1)} %get-tuple-element.59, f32[4608]{0:T(1024)S(1)} %get-tuple-element.57, ...), channel_id=5, replica_groups=mesh['clip'=8,'frame'=4] {'frame'}, use_global_device_ids=true, to_apply=%region_21.22.clone | all-reduce | flops 9216 | bytes 73728
  788.2 26.7 %all-reduce.4 = (f32[576]{0:T(1024)}, f32[288]{0:T(512)}, f32[1152]{0:T(1024)}, f32[288]{0:T(512)}) all-reduce(f32[576]{0:T(1024)S(1)} %dynamic-slice.1, f32[288]{0:T(512)S(1)} %dynamic-slice.3, f32[1152]{0:T(1024)S(1)} %dynamic-slice.5, f32[288]{0:T(512)S(1)} %dynamic-slice.7), channel_id=1, replica_groups=mesh['clip'=8,'frame'=4] {'clip'}, use_global_device_ids=true, to_apply=%region_22.23 | all-reduce | flops 2304 | bytes 18432 | tf_op jit(solution)/shard_map/psum | solution.py:205
  814.9 2.1 copy.81
  816.9 2.5 copy.73
  819.5 2.4 copy.65
  821.9 51.5 %reduce-scatter.34.cloned.1.call-done = f32[576,288]{1,0:T(8,128)} async-done(((f32[4608,288]{1,0:T(8,128)}), f32[576,288]{1,0:T(8,128)}) %reduce-scatter.34.cloned.1.call-update) | async-done | bytes 663568
  873.4 2.3 copy.87
  875.7 33.6 %reduce-scatter.32.cloned.1.call-done = f32[144,288]{1,0:T(8,128)} async-done(((f32[1152,288]{1,0:T(8,128)}), f32[144,288]{1,0:T(8,128)}) %reduce-scatter.32.cloned.1.call-update) | async-done | bytes 165904
  909.3 50.7 %reduce-scatter.30.cloned.1.call-done = f32[144,864]{1,0:T(8,128)} async-done(((f32[1152,864]{1,0:T(8,128)}), f32[144,864]{1,0:T(8,128)}) %reduce-scatter.30.cloned.1.call-update) | async-done | bytes 497680
  960.0 61.6 %reduce-scatter.24.cloned.1.call-done = f32[144,1152]{1,0:T(8,128)} async-done(((f32[1152,1152]{1,0:T(8,128)}), f32[144,1152]{1,0:T(8,128)}) %reduce-scatter.24.cloned.1.call-update) | async-done | bytes 663568 | tf_op jit(solution)/shard_map/reduce_scatter | solution.py:196
  (177 shorter events, 23.8 us)
Async XLA Ops:
  7.2 79.0 %copy-start = (bf16[1152,1152]{1,0:T(8,128)(2,1)S(1)}, bf16[1152,1152]{1,0:T(8,128)(2,1)}, u32[]{:S(2)}) copy-start(bf16[1152,1152]{1,0:T(8,128)(2,1)} %param.17) | copy-start | bytes 7962628
  7.2 8.7 copy-start.37
  7.2 8.8 copy-start.38
  7.2 8.8 copy-start.44
  7.2 8.9 copy-start.42
  10.6 8.9 copy-start.39
  10.6 21.0 %all-to-all-start = ((bf16[2,4,64,1152]{3,1,0,2:T(4,128)(2,1)}), bf16[2,4,64,1152]{3,1,0,2:T(4,128)(2,1)}, u32[]{:S(2)}, u32[]{:S(2)}) async-start(bf16[2,4,64,1152]{3,1,0,2:T(4,128)(2,1)} %copy.57), calls=%async_computation | async-start | bytes 2359296 | tf_op jit(solution)/shard_map/all_to_all | solution.py:51
  16.1 15.5 %copy-start.40 = (f32[2,16]{1,0:T(2,128)}, f32[2,16]{1,0:T(2,128)S(1)}, u32[]{:S(2)}) copy-start(f32[2,16]{1,0:T(2,128)S(1)} %get-tuple-element.97) | copy-start | bytes 388
  19.5 22.2 %copy-start.34 = (f32[2,1152]{1,0:T(2,128)}, f32[2,1152]{1,0:T(2,128)S(1)}, u32[]{:S(2)}) copy-start(f32[2,1152]{1,0:T(2,128)S(1)} %get-tuple-element.106) | copy-start | bytes 27652
  31.6 62.3 %all-to-all-start.2 = ((bf16[2,4,64,1152]{3,1,0,2:T(4,128)(2,1)}), bf16[2,4,64,1152]{3,1,0,2:T(4,128)(2,1)}, u32[]{:S(2)}, u32[]{:S(2)}) async-start(bf16[2,4,64,1152]{3,1,0,2:T(4,128)(2,1)} %copy.66), calls=%async_computation.2 | async-start | bytes 2359296 | tf_op jit(solution)/shard_map/all_to_all | solution.py:114
  35.9 279.5 %reduce-scatter.26.cloned.1.call-start = ((), (), s32[]{:S(2)}) async-start(), calls=%async_computation.17 | async-start | bytes 26542080 | tf_op jit(solution)/shard_map/reduce_scatter | solution.py:186
  37.5 1.4 copy-start.7
  41.7 1.4 copy-start.2
  72.4 2.6 copy-start.15
  72.4 2.6 copy-start.17
  72.4 4.9 copy-start.32
  77.3 1.9 copy-start.27
  86.2 3.3 copy-start.8
  89.5 2.2 copy-start.5
  93.9 2.0 copy-start.3
  95.6 12.9 %copy-start.9 = (f32[2,4,4,16,1152]{4,3,1,2,0:T(8,128)}, f32[2,4,4,16,1152]{4,3,1,2,0:T(8,128)S(1)}, u32[]{:S(2)}) copy-start(f32[2,4,4,16,1152]{4,3,1,2,0:T(8,128)S(1)} %copy.67) | copy-start | bytes 7077892
  98.8 9.5 copy-start.22
  108.4 3.7 copy-start.47
  112.1 1.0 copy-start.33
  123.4 0.7 copy-start.43
  123.5 257.3 %reduce-scatter.20.cloned.1.call-start = ((), (), s32[]{:S(2)}) async-start(), calls=%async_computation.14 | async-start | bytes 6635520 | tf_op jit(solution)/shard_map/reduce_scatter | solution.py:184
  139.9 11.1 %copy-start.21 = (bf16[512,4608]{1,0:T(8,128)(2,1)}, bf16[512,4608]{1,0:T(8,128)(2,1)S(1)}, u32[]{:S(2)}) copy-start(bf16[512,4608]{1,0:T(8,128)(2,1)S(1)} %get-tuple-element.58) | copy-start | bytes 14155780
  139.9 12.5 %copy-start.14 = (f32[2,4,4,16,1152]{4,3,2,1,0:T(8,128)S(1)}, f32[2,4,4,16,1152]{4,3,2,1,0:T(8,128)}, u32[]{:S(2)}) copy-start(f32[2,4,4,16,1152]{4,3,2,1,0:T(8,128)} %get-tuple-element.69) | copy-start | bytes 7077892
  151.0 1.4 copy-start.12
  153.0 4.3 copy-start.10
  157.3 1.6 copy-start.19
  157.9 1.0 copy-start.26
  163.0 368.5 %reduce-scatter.18.cloned.1.call-start = ((), (), s32[]{:S(2)}) async-start(), calls=%async_computation.13 | async-start | bytes 19906560 | tf_op jit(solution)/shard_map/reduce_scatter | solution.py:183
  172.5 7.2 copy-start.30
  172.5 7.2 copy-start.28
  179.7 1.6 copy-start.18
  181.3 1.9 copy-start.16
  183.2 1.7 copy-start.31
  204.3 11.0 %copy-start.4 = (f32[2,4,4,16,1152]{4,3,1,2,0:T(8,128)S(1)}, f32[2,4,4,16,1152]{4,3,1,2,0:T(8,128)}, u32[]{:S(2)}) copy-start(f32[2,4,4,16,1152]{4,3,1,2,0:T(8,128)} %copy-done.2) | copy-start | bytes 7077892
  215.3 9.9 copy-start.36
  215.3 9.9 copy-start.6
  215.3 9.9 copy-start.13
  227.2 13.7 %copy-start.11 = (f32[2,4,4,16,1152]{4,3,1,2,0:T(8,128)S(1)}, f32[2,4,4,16,1152]{4,3,1,2,0:T(8,128)}, u32[]{:S(2)}) copy-start(f32[2,4,4,16,1152]{4,3,1,2,0:T(8,128)} %copy-done.9) | copy-start | bytes 7077892
  227.2 13.7 %copy-start.41 = (f32[2,16]{1,0:T(2,128)S(1)}, f32[2,16]{1,0:T(2,128)}, u32[]{:S(2)}) copy-start(f32[2,16]{1,0:T(2,128)} %copy-done.40) | copy-start | bytes 388
  240.9 2.7 copy-start.35
  243.6 2.2 copy-start.29
  254.2 1.6 copy-start.23
  254.2 470.2 %reduce-scatter.22.cloned.1.call-start = ((), (), s32[]{:S(2)}) async-start(), calls=%async_computation.15 | async-start | bytes 26542080 | tf_op jit(solution)/shard_map/reduce_scatter | solution.py:185
  268.0 546.8 %reduce-scatter.28.cloned.1.call-start = ((), (), s32[]{:S(2)}) async-start(), calls=%async_computation.18 | async-start | bytes 4423680
  271.0 602.4 %reduce-scatter.34.cloned.1.call-start = ((), (), s32[]{:S(2)}) async-start(), calls=%async_computation.21 | async-start | bytes 7962624
  322.1 587.2 %reduce-scatter.32.cloned.1.call-start = ((), (), s32[]{:S(2)}) async-start(), calls=%async_computation.20 | async-start | bytes 1990656
  383.8 576.1 %reduce-scatter.30.cloned.1.call-start = ((), (), s32[]{:S(2)}) async-start(), calls=%async_computation.19 | async-start | bytes 4644864
  537.0 484.5 %reduce-scatter.24.cloned.1.call-start = ((), (), s32[]{:S(2)}) async-start(), calls=%async_computation.16 | async-start | bytes 5971968 | tf_op jit(solution)/shard_map/reduce_scatter | solution.py:196
  724.4 1.3 copy-start.25
  725.6 4.7 copy-start.46
  725.6 7.2 copy-start.45
  725.6 7.5 copy-start.20
  726.8 29.1 %all-to-all-start.3 = ((bf16[2,16,16,1152]{3,2,0,1:T(8,128)(2,1)}), bf16[2,16,16,1152]{3,2,0,1:T(8,128)(2,1)S(1)}, u32[]{:S(2)}, u32[]{:S(2)}) async-start(bf16[2,16,16,1152]{3,2,0,1:T(8,128)(2,1)} %copy.72), calls=%async_computation.3 | async-start | bytes 2359296 | tf_op jit(solution)/shard_map/all_to_all | solution.py:168
  755.9 4.3 copy-start.24
  755.9 63.6 %all-to-all-start.1 = ((bf16[2,16,16,1152]{3,2,0,1:T(8,128)(2,1)}), bf16[2,16,16,1152]{3,2,0,1:T(8,128)(2,1)}, u32[]{:S(2)}, u32[]{:S(2)}) async-start(bf16[2,16,16,1152]{3,2,0,1:T(8,128)(2,1)} %copy.64), calls=%async_computation.1 | async-start | bytes 2359296 | tf_op jit(solution)/shard_map/all_to_all | solution.py:111
  816.9 204.6 %copy-start.1 = (bf16[1152,1152]{1,0:T(8,128)(2,1)S(1)}, bf16[1152,1152]{1,0:T(8,128)(2,1)}, u32[]{:S(2)}) copy-start(bf16[1152,1152]{1,0:T(8,128)(2,1)} %param.17) | copy-start | bytes 7962628
Sparse Core Ops, SparseCore 0:
  123.6 191.7 reduce-scatter.25
  318.7 61.9 reduce-scatter.19
  384.1 147.2 reduce-scatter.17
  534.4 189.9 reduce-scatter.21
  727.6 65.9 reduce-scatter.27
  795.9 77.4 reduce-scatter.33
  876.3 32.9 reduce-scatter.31
  912.3 47.6 reduce-scatter.29
  962.9 58.6 reduce-scatter.23
where the time goes:
time: 1030 us
  waiting for transfers between devices  669 us (65%)
  matrix products  129 us (13%)
  local copies, waits for them, and re-layouts  112 us (11%)
  blocking collectives  52.1 us (5%)
  other arithmetic  31.5 us (3%)
  starting transfers between devices  17.8 us (2%)
  between operations  16.9 us (2%)
    reduce_scatter x1, waiting for transfers between devices, on_device(): lax.psum_scatter(d_fc1_weight, 'frame', scatter_dimension=1, tiled=True)  187 us
    reduce_scatter x1, waiting for transfers between devices, on_device(): lax.psum_scatter(d_qkv_weight, 'frame', scatter_dimension=1, tiled=True)  148 us
    unnamed x13, waiting for transfers between devices  136 us
    reduce_scatter x1, waiting for transfers between devices, on_device(): lax.psum_scatter(every_part[2], 'clip', scatter_dimension=0, tiled=True)  61.6 us
    reduce_scatter x1, waiting for transfers between devices, on_device(): lax.psum_scatter(d_out_weight, 'frame', scatter_dimension=1, tiled=True)  58.5 us
    reduce_scatter x1, waiting for transfers between devices, on_device(): lax.psum_scatter(d_fc2_weight, 'frame', scatter_dimension=1, tiled=True)  44.4 us
    unnamed x113, local copies, waits for them, and re-layouts  43.8 us
    dot_general x4, matrix products, contract_cols(): lax.dot_general(left, right, (((1,), (1,)), ((), ())), preferred_element_...  40.8 us
  transfers between devices with their start and end apart: 13, of which 10 were waited for; matrix products, arithmetic and copies ran while one was open for 22% of the time, Pallas kernels for 0%

commit v1 on v0

--- a/solution.py
+++ b/solution.py
@@ -165,9 +165,21 @@
     )
     d_residual, d_shift_one, d_scale_one = modulate_back_one(d_normed_one)
     d_input = d_middle + d_residual
-    input_grad = lax.all_to_all(
-        d_input.astype(jnp.bfloat16), "frame", split_axis=1, concat_axis=2, tiled=True
-    )
+    x = d_input.astype(jnp.bfloat16)
+    ways, here = (lax.axis_size("frame"), lax.axis_index("frame"))
+    width = x.shape[1] // ways
+    shape = list(x.shape)
+    shape[1] = width
+    height = shape[2]
+    shape[2] = height * ways
+    input_grad = jnp.zeros(shape, x.dtype)
+    for mask in range(ways):
+        part = lax.dynamic_slice_in_dim(x, (here ^ mask) * width, width, axis=1)
+        if mask:
+            part = lax.ppermute(part, "frame", [(d, d ^ mask) for d in range(ways)])
+        input_grad = lax.dynamic_update_slice_in_dim(
+            input_grad, part, (here ^ mask) * height, axis=2
+        )
     d_modulation = jnp.stack(
         [
             d_shift_one.reshape(clip_count, model_width),

time: 1030 us -> 1030 us (level)
  waiting for transfers between devices: 669 us -> 654 us
  blocking collectives: 52.1 us -> 65.4 us
    all_to_all x1 -> x0, waiting for transfers between devices: 21.7 us -> none  [on_device(): lax.all_to_all(d_input.astype(jnp.bfloat16), 'frame', split_axis=1, conca...]
    unnamed x1, blocking collectives: 25.4 us -> 38.9 us
    unnamed x113 -> x115, local copies, waits for them, and re-layouts: 43.8 us -> 43.9 us
  transfers between devices with their start and end apart: 13 -> 15, of which waited for: 10 -> 9; matrix products, arithmetic and copies ran while one was open for 22% -> 23% of each run, Pallas kernels for 0% -> 0%
where the time goes in v1:
time: 1030 us
  waiting for transfers between devices  654 us (63%)
  matrix products  129 us (13%)
  local copies, waits for them, and re-layouts  113 us (11%)
  blocking collectives  65.4 us (6%)
  other arithmetic  33 us (3%)
  between operations  16.9 us (2%)
  starting transfers between devices  16.3 us (2%)
    reduce_scatter x1, waiting for transfers between devices, on_device(): lax.psum_scatter(d_fc1_weight, 'frame', scatter_dimension=1, tiled=True)  187 us
    reduce_scatter x1, waiting for transfers between devices, on_device(): lax.psum_scatter(d_qkv_weight, 'frame', scatter_dimension=1, tiled=True)  148 us
    unnamed x13, waiting for transfers between devices  144 us
    reduce_scatter x1, waiting for transfers between devices, on_device(): lax.psum_scatter(every_part[2], 'clip', scatter_dimension=0, tiled=True)  61.6 us
    reduce_scatter x1, waiting for transfers between devices, on_device(): lax.psum_scatter(d_out_weight, 'frame', scatter_dimension=1, tiled=True)  58.5 us
    unnamed x115, local copies, waits for them, and re-layouts  43.9 us
    reduce_scatter x1, waiting for transfers between devices, on_device(): lax.psum_scatter(d_fc2_weight, 'frame', scatter_dimension=1, tiled=True)  43.2 us
    dot_general x4, matrix products, contract_cols(): lax.dot_general(left, right, (((1,), (1,)), ((), ())), preferred_element_...  41.5 us
  transfers between devices with their start and end apart: 15, of which 9 were waited for; matrix products, arithmetic and copies ran while one was open for 23% of the time, Pallas kernels for 0%

profile of v1, /device:TPU:0, one launch (start us, length us, event | category | flops | bytes accessed | tf_op | source)
XLA Modules:
  0.0 1028.5 jit_solution(10134538719304925673)
XLA Ops:
  7.2 3.3 copy.55
  10.6 5.3 all-to-all-start
  16.1 3.2 copy.64
  19.6 12.0 %all-to-all-done = bf16[2,4,64,1152]{3,1,0,2:T(4,128)(2,1)} async-done(((bf16[2,4,64,1152]{3,1,0,2:T(4,128)(2,1)}), bf16[2,4,64,1152]{3,1,0,2:T(4,128)(2,1)}, u32[]{:S(2)}, u32[]{:S(2)}) %all-to-all-start) | async-done | bytes 1179680 | tf_op jit(solution)/shard_map/all_to_all | solution.py:51
  31.6 4.3 all-to-all-start.2
  35.9 1.6 bitcast_convert_fusion.1
  43.7 10.0 add_convert_fusion
  53.7 13.6 %reshape.417 = bf16[2,16,16,3,16,72]{5,4,3,2,1,0:T(8,128)(2,1)} reshape(bf16[512,3456]{1,0:T(8,128)(2,1)} %add_convert_fusion) | data formatting | bytes 7077888 | tf_op jit(solution)/shard_map/reshape | solution.py:77
  67.3 5.0 fusion.48
  72.4 2.5 fusion.33
  74.9 2.4 fusion.52
  77.3 1.8 convert_bitcast_fusion
  79.2 1.9 copy.61
  81.1 5.1 reshape.418
  86.2 3.3 convolution_add_fusion.1
  89.5 2.1 fusion.47
  91.7 2.0 multiply_reduce_fusion.6
  93.9 1.6 copy.65
  95.9 2.9 fusion.17
  98.8 9.5 fusion.53
  108.7 3.4 copy-done.48
  113.0 10.4 %fusion.42 = f32[4608,1152]{0,1:T(8,128)} fusion(bf16[512,1152]{1,0:T(8,128)(2,1)S(1)} %fusion.19, f32[512,4608]{1,0:T(8,128)S(1)} %fusion.53, f32[4608]{0:T(1024)S(1)} %convert_element_type.207), kind=kOutput, calls=%fused_computation.122 | convolution fusion | flops 5459410944 | bytes 31868928 | tf_op jit(solution)/shard_map/dot_general | solution.py:26
  124.1 16.4 %convert_reduce_fusion.1 = (f32[4608]{0:T(1024)}, bf16[512,4608]{1,0:T(8,128)(2,1)S(1)}) fusion(f32[512,4608]{1,0:T(8,128)} %copy-done.48, f32[4608]{0:T(1024)S(1)} %convert_element_type.207, bf16[512,1152]{1,0:T(8,128)(2,1)} %copy-done.32, bf16[4608,1152]{1,0:T(8,128)(2,1)} %param.21), kind=kOutput, calls=%fused_computation.12 | convolution fusion | flops 5490077184 | bytes 25989120 | tf_op jit(solution)/shard_map/dot_general | solution.py:32
  140.5 10.9 %fusion.54 = f32[512,1152]{1,0:T(8,128)S(1)} fusion(bf16[512,4608]{1,0:T(8,128)(2,1)S(1)} %get-tuple-element.58, bf16[1152,4608]{1,0:T(8,128)(2,1)} %param.19), kind=kOutput, calls=%fused_computation.133 | convolution fusion | flops 5435817984 | bytes 17694720 | tf_op jit(solution)/shard_map/dot_general | solution.py:32
  153.4 4.1 fusion.46
  159.8 4.1 fusion.56
  163.9 4.3 convolution_convert_fusion
  168.3 5.2 reshape.424
  173.5 7.0 multiply_reduce_fusion
  182.1 1.7 multiply_bitcast_fusion.1
  183.9 1.7 multiply_bitcast_fusion
  185.6 1.6 convolution_bitcast_fusion
  187.2 2.8 convert_reduce_fusion
  190.0 4.2 copy.69
  194.3 11.3 %convert_element_type.223 = bf16[2,16,16,3456]{3,2,1,0:T(8,128)(2,1)} reshape(bf16[2,16,16,3,16,72]{5,4,3,2,1,0:T(8,128)(2,1)} %copy.69) | data formatting | bytes 7077888 | tf_op jit(solution)/shard_map/convert_element_type | solution.py:157
  205.6 11.0 %convert_element_type.227 = bf16[512,3456]{1,0:T(8,128)(2,1)} reshape(bf16[2,16,16,3,16,72]{5,4,3,2,1,0:T(8,128)(2,1)} %copy.69) | data formatting | bytes 7077888 | tf_op jit(solution)/shard_map/convert_element_type | solution.py:157
  216.7 9.9 multiply_reduce_fusion.4
  226.6 2.0 multiply_reduce_fusion.3
  228.6 13.3 %convolution_add_fusion = f32[512,1152]{1,0:T(8,128)S(1)} fusion(bf16[4608,1152]{1,0:T(8,128)(2,1)} %param.21, f32[1152]{0:T(1024)S(1)} %convert_element_type.209, f32[512,4608]{1,0:T(8,128)} %copy-done.48, f32[4608]{0:T(1024)S(1)} %convert_element_type.207), kind=kOutput, calls=%fused_computation.30 | convolution fusion | flops 5460000768 | bytes 22436352 | tf_op jit(solution)/shard_map/dot_general | solution.py:106
  242.0 2.7 multiply_reduce_fusion.2
  244.7 2.1 add_convert_fusion.1
  247.1 8.7 fusion.55
  257.1 12.2 %fusion.57 = f32[1152,4608]{1,0:T(8,128)} fusion(bf16[512,1152]{1,0:T(8,128)(2,1)S(1)} %copy-done.23, bf16[512,4608]{1,0:T(8,128)(2,1)} %copy-done.21), kind=kOutput, calls=%fused_computation.136 | convolution fusion | flops 5435817984 | bytes 27131904 | tf_op jit(solution)/shard_map/dot_general | solution.py:26
  269.5 2.7 copy.84
  272.3 43.2 %reduce-scatter.26.cloned.1.call-done = f32[4608,288]{0,1:T(8,128)} async-done(((f32[4608,1152]{0,1:T(8,128)}), f32[4608,288]{0,1:T(8,128)}) %reduce-scatter.26.cloned.1.call-update) | async-done | bytes 5308432 | tf_op jit(solution)/shard_map/reduce_scatter | solution.py:198
  315.4 6.7 copy.82
  322.2 58.5 %reduce-scatter.20.cloned.1.call-done = f32[1152,288]{0,1:T(8,128)} async-done(((f32[1152,1152]{0,1:T(8,128)}), f32[1152,288]{0,1:T(8,128)}) %reduce-scatter.20.cloned.1.call-update) | async-done | bytes 1327120 | tf_op jit(solution)/shard_map/reduce_scatter | solution.py:196
  380.8 3.1 copy.80
  383.9 147.5 %reduce-scatter.18.cloned.1.call-done = f32[1152,864]{0,1:T(8,128)} async-done(((f32[1152,3456]{0,1:T(8,128)}), f32[1152,864]{0,1:T(8,128)}) %reduce-scatter.18.cloned.1.call-update) | async-done | bytes 3981328 | tf_op jit(solution)/shard_map/reduce_scatter | solution.py:195
  531.5 5.6 copy.78
  537.1 187.3 %reduce-scatter.22.cloned.1.call-done = f32[1152,1152]{1,0:T(8,128)} async-done(((f32[1152,4608]{1,0:T(8,128)}), f32[1152,1152]{1,0:T(8,128)}) %reduce-scatter.22.cloned.1.call-update) | async-done | bytes 5308432 | tf_op jit(solution)/shard_map/reduce_scatter | solution.py:197
  732.1 4.3 all-to-all-start.1
  736.5 1.6 bitcast_convert_fusion
  739.4 38.9 %all-reduce.5 = (f32[2304]{0:T(1024)S(1)}, f32[1152]{0:T(1024)S(1)}, f32[4608]{0:T(1024)S(1)}, f32[1152]{0:T(1024)S(1)}) all-reduce(f32[2304]{0:T(1024)S(1)} %pad_maximum_fusion, f32[1152]{0:T(1024)} %get-tuple-element.59, f32[4608]{0:T(1024)} %get-tuple-element.57, ...), channel_id=5, replica_groups=mesh['clip'=8,'frame'=4] {'frame'}, use_global_device_ids=true, to_apply=%region_21.22.clone | all-reduce | flops 9216 | bytes 73728
  778.6 26.5 %all-reduce.4 = (f32[576]{0:T(1024)}, f32[288]{0:T(512)}, f32[1152]{0:T(1024)}, f32[288]{0:T(512)}) all-reduce(f32[576]{0:T(1024)S(1)} %dynamic-slice.1, f32[288]{0:T(512)S(1)} %dynamic-slice.3, f32[1152]{0:T(1024)S(1)} %dynamic-slice.5, f32[288]{0:T(512)S(1)} %dynamic-slice.7), channel_id=1, replica_groups=mesh['clip'=8,'frame'=4] {'clip'}, use_global_device_ids=true, to_apply=%region_22.23 | all-reduce | flops 2304 | bytes 18432 | tf_op jit(solution)/shard_map/psum | solution.py:217
  805.1 2.1 copy.77
  807.1 1.7 constant_dynamic-update-slice_fusion.1
  809.6 1.9 constant_dynamic-update-slice_fusion.2
  811.5 2.4 copy.63
  813.9 59.5 %reduce-scatter.34.cloned.1.call-done = f32[576,288]{1,0:T(8,128)} async-done(((f32[4608,288]{1,0:T(8,128)}), f32[576,288]{1,0:T(8,128)}) %reduce-scatter.34.cloned.1.call-update) | async-done | bytes 663568
  873.4 2.3 copy.83
  875.7 33.8 %reduce-scatter.32.cloned.1.call-done = f32[144,288]{1,0:T(8,128)} async-done(((f32[1152,288]{1,0:T(8,128)}), f32[144,288]{1,0:T(8,128)}) %reduce-scatter.32.cloned.1.call-update) | async-done | bytes 165904
  909.5 50.7 %reduce-scatter.30.cloned.1.call-done = f32[144,864]{1,0:T(8,128)} async-done(((f32[1152,864]{1,0:T(8,128)}), f32[144,864]{1,0:T(8,128)}) %reduce-scatter.30.cloned.1.call-update) | async-done | bytes 497680
  960.2 61.6 %reduce-scatter.24.cloned.1.call-done = f32[144,1152]{1,0:T(8,128)} async-done(((f32[1152,1152]{1,0:T(8,128)}), f32[144,1152]{1,0:T(8,128)}) %reduce-scatter.24.cloned.1.call-update) | async-done | bytes 663568 | tf_op jit(solution)/shard_map/reduce_scatter | solution.py:208
  (186 shorter events, 25.3 us)
Async XLA Ops:
  7.2 79.0 %copy-start = (bf16[1152,1152]{1,0:T(8,128)(2,1)S(1)}, bf16[1152,1152]{1,0:T(8,128)(2,1)}, u32[]{:S(2)}) copy-start(bf16[1152,1152]{1,0:T(8,128)(2,1)} %param.17) | copy-start | bytes 7962628
  7.2 8.7 copy-start.38
  7.2 8.8 copy-start.39
  7.2 8.8 copy-start.45
  7.2 8.9 copy-start.43
  10.6 8.9 copy-start.40
  10.6 21.0 %all-to-all-start = ((bf16[2,4,64,1152]{3,1,0,2:T(4,128)(2,1)}), bf16[2,4,64,1152]{3,1,0,2:T(4,128)(2,1)}, u32[]{:S(2)}, u32[]{:S(2)}) async-start(bf16[2,4,64,1152]{3,1,0,2:T(4,128)(2,1)} %copy.55), calls=%async_computation | async-start | bytes 2359296 | tf_op jit(solution)/shard_map/all_to_all | solution.py:51
  16.1 15.5 %copy-start.41 = (f32[2,16]{1,0:T(2,128)}, f32[2,16]{1,0:T(2,128)S(1)}, u32[]{:S(2)}) copy-start(f32[2,16]{1,0:T(2,128)S(1)} %get-tuple-element.101) | copy-start | bytes 388
  19.5 22.1 %copy-start.34 = (f32[2,1152]{1,0:T(2,128)}, f32[2,1152]{1,0:T(2,128)S(1)}, u32[]{:S(2)}) copy-start(f32[2,1152]{1,0:T(2,128)S(1)} %get-tuple-element.110) | copy-start | bytes 27652
  31.6 62.3 %all-to-all-start.2 = ((bf16[2,4,64,1152]{3,1,0,2:T(4,128)(2,1)}), bf16[2,4,64,1152]{3,1,0,2:T(4,128)(2,1)}, u32[]{:S(2)}, u32[]{:S(2)}) async-start(bf16[2,4,64,1152]{3,1,0,2:T(4,128)(2,1)} %copy.64), calls=%async_computation.2 | async-start | bytes 2359296 | tf_op jit(solution)/shard_map/all_to_all | solution.py:114
  35.9 279.6 %reduce-scatter.26.cloned.1.call-start = ((), (), s32[]{:S(2)}) async-start(), calls=%async_computation.16 | async-start | bytes 26542080 | tf_op jit(solution)/shard_map/reduce_scatter | solution.py:198
  37.5 1.4 copy-start.7
  41.7 1.4 copy-start.2
  72.3 2.6 copy-start.15
  72.3 2.6 copy-start.17
  72.3 4.9 copy-start.31
  77.3 1.9 copy-start.26
  86.2 3.3 copy-start.8
  89.4 2.2 copy-start.5
  93.9 2.0 copy-start.3
  95.5 12.9 %copy-start.9 = (f32[2,4,4,16,1152]{4,3,1,2,0:T(8,128)}, f32[2,4,4,16,1152]{4,3,1,2,0:T(8,128)S(1)}, u32[]{:S(2)}) copy-start(f32[2,4,4,16,1152]{4,3,1,2,0:T(8,128)S(1)} %copy.65) | copy-start | bytes 7077892
  98.8 9.5 copy-start.22
  108.4 3.7 copy-start.48
  112.0 1.0 copy-start.32
  123.4 0.7 copy-start.44
  123.5 257.3 %reduce-scatter.20.cloned.1.call-start = ((), (), s32[]{:S(2)}) async-start(), calls=%async_computation.13 | async-start | bytes 6635520 | tf_op jit(solution)/shard_map/reduce_scatter | solution.py:196
  140.5 10.9 %copy-start.21 = (bf16[512,4608]{1,0:T(8,128)(2,1)}, bf16[512,4608]{1,0:T(8,128)(2,1)S(1)}, u32[]{:S(2)}) copy-start(bf16[512,4608]{1,0:T(8,128)(2,1)S(1)} %get-tuple-element.58) | copy-start | bytes 14155780
  140.5 12.3 %copy-start.14 = (f32[2,4,4,16,1152]{4,3,2,1,0:T(8,128)S(1)}, f32[2,4,4,16,1152]{4,3,2,1,0:T(8,128)}, u32[]{:S(2)}) copy-start(f32[2,4,4,16,1152]{4,3,2,1,0:T(8,128)} %get-tuple-element.69) | copy-start | bytes 7077892
  151.5 1.4 copy-start.12
  153.4 4.2 copy-start.10
  157.6 2.2 copy-start.19
  158.8 1.0 copy-start.25
  163.9 367.6 %reduce-scatter.18.cloned.1.call-start = ((), (), s32[]{:S(2)}) async-start(), calls=%async_computation.12 | async-start | bytes 19906560 | tf_op jit(solution)/shard_map/reduce_scatter | solution.py:195
  173.5 7.0 copy-start.29
  173.5 7.0 copy-start.27
  180.5 1.6 copy-start.18
  182.1 1.7 copy-start.16
  183.8 1.7 copy-start.30
  205.6 11.1 %copy-start.4 = (f32[2,4,4,16,1152]{4,3,1,2,0:T(8,128)S(1)}, f32[2,4,4,16,1152]{4,3,1,2,0:T(8,128)}, u32[]{:S(2)}) copy-start(f32[2,4,4,16,1152]{4,3,1,2,0:T(8,128)} %copy-done.2) | copy-start | bytes 7077892
  216.6 9.9 copy-start.37
  216.6 10.0 copy-start.6
  216.6 10.0 copy-start.13
  228.6 13.3 %copy-start.11 = (f32[2,4,4,16,1152]{4,3,1,2,0:T(8,128)S(1)}, f32[2,4,4,16,1152]{4,3,1,2,0:T(8,128)}, u32[]{:S(2)}) copy-start(f32[2,4,4,16,1152]{4,3,1,2,0:T(8,128)} %copy-done.9) | copy-start | bytes 7077892
  228.6 13.3 %copy-start.42 = (f32[2,16]{1,0:T(2,128)S(1)}, f32[2,16]{1,0:T(2,128)}, u32[]{:S(2)}) copy-start(f32[2,16]{1,0:T(2,128)} %copy-done.41) | copy-start | bytes 388
  242.0 2.7 copy-start.35
  244.7 2.5 copy-start.28
  255.8 1.3 copy-start.23
  255.8 468.5 %reduce-scatter.22.cloned.1.call-start = ((), (), s32[]{:S(2)}) async-start(), calls=%async_computation.14 | async-start | bytes 26542080 | tf_op jit(solution)/shard_map/reduce_scatter | solution.py:197
  269.3 535.8 %reduce-scatter.28.cloned.1.call-start = ((), (), s32[]{:S(2)}) async-start(), calls=%async_computation.17 | async-start | bytes 4423680
  272.2 601.1 %reduce-scatter.34.cloned.1.call-start = ((), (), s32[]{:S(2)}) async-start(), calls=%async_computation.20 | async-start | bytes 7962624
  322.2 587.3 %reduce-scatter.32.cloned.1.call-start = ((), (), s32[]{:S(2)}) async-start(), calls=%async_computation.19 | async-start | bytes 1990656
  383.9 576.3 %reduce-scatter.30.cloned.1.call-start = ((), (), s32[]{:S(2)}) async-start(), calls=%async_computation.18 | async-start | bytes 4644864
  537.1 484.7 %reduce-scatter.24.cloned.1.call-start = ((), (), s32[]{:S(2)}) async-start(), calls=%async_computation.15 | async-start | bytes 5971968 | tf_op jit(solution)/shard_map/reduce_scatter | solution.py:208
  724.4 0.7 copy-start.47
  724.4 3.2 copy-start.46
  724.4 3.4 copy-start.24
  724.4 6.6 copy-start.20
  728.0 1.0 copy-start.33
  729.0 78.1 %collective-permute-start = (bf16[2,4,16,1152]{3,2,1,0:T(8,128)(2,1)S(1)}, bf16[2,4,16,1152]{3,2,1,0:T(8,128)(2,1)}, u32[]{:S(2)}, u32[]{:S(2)}) collective-permute-start(bf16[2,4,16,1152]{3,2,1,0:T(8,128)(2,1)S(1)} %get-tuple-element.82), channel_id=1, source_target_pairs={{0,1},{1,0},{2,3},{3,2},{4,5},{5,4},{6,7},{7,6},{8,9},{9,8},{10,11... | collective-permute-start | bytes 884744 | tf_op jit(solution)/shard_map/ppermute | solution.py:179
  730.4 78.5 %collective-permute-start.1 = (bf16[2,4,16,1152]{3,2,1,0:T(8,128)(2,1)S(1)}, bf16[2,4,16,1152]{3,2,1,0:T(8,128)(2,1)S(1)}, u32[]{:S(2)}, u32[]{:S(2)}) collective-permute-start(bf16[2,4,16,1152]{3,2,1,0:T(8,128)(2,1)S(1)} %get-tuple-element.81), channel_id=1, source_target_pairs={{0,2},{1,3},{2,0},{3,1},{4,6},{5,7},{6,4},{7,5},{8,10},{9,11},{10,... | collective-permute-start | bytes 884744 | tf_op jit(solution)/shard_map/ppermute | solution.py:179
  732.1 79.4 %all-to-all-start.1 = ((bf16[2,16,16,1152]{3,2,0,1:T(8,128)(2,1)}), bf16[2,16,16,1152]{3,2,0,1:T(8,128)(2,1)}, u32[]{:S(2)}, u32[]{:S(2)}) async-start(bf16[2,16,16,1152]{3,2,0,1:T(8,128)(2,1)} %copy.62), calls=%async_computation.1 | async-start | bytes 2359296 | tf_op jit(solution)/shard_map/all_to_all | solution.py:111
  736.5 2.7 copy-start.36
  778.4 31.2 %collective-permute-start.2 = (bf16[2,4,16,1152]{3,2,1,0:T(8,128)(2,1)S(1)}, bf16[2,4,16,1152]{3,2,1,0:T(8,128)(2,1)}, u32[]{:S(2)}, u32[]{:S(2)}) collective-permute-start(bf16[2,4,16,1152]{3,2,1,0:T(8,128)(2,1)S(1)} %get-tuple-element.80), channel_id=1, source_target_pairs={{0,3},{1,2},{2,1},{3,0},{4,7},{5,6},{6,5},{7,4},{8,11},{9,10},{10,... | collective-permute-start | bytes 884744 | tf_op jit(solution)/shard_map/ppermute | solution.py:179
  808.8 213.0 %copy-start.1 = (bf16[1152,1152]{1,0:T(8,128)(2,1)S(1)}, bf16[1152,1152]{1,0:T(8,128)(2,1)}, u32[]{:S(2)}) copy-start(bf16[1152,1152]{1,0:T(8,128)(2,1)} %param.17) | copy-start | bytes 7962628
Sparse Core Ops, SparseCore 0:
  123.6 191.8 reduce-scatter.25
  318.7 61.9 reduce-scatter.19
  384.2 147.2 reduce-scatter.17
  534.4 189.9 reduce-scatter.21
  727.6 66.7 reduce-scatter.27
  796.7 76.6 reduce-scatter.33
  876.4 33.1 reduce-scatter.31
  912.5 47.6 reduce-scatter.29
  963.1 58.6 reduce-scatter.23
